TPU v7x, 128 devices: a whole 4x4x4 slice. The times are simulated.
128 devices in a mesh: dp: 16 (over y, z), mp: 8 (over x, core).
Axes of the slice: x: 4, y: 4, z: 4, core: 2. Of those that a mesh axis runs over, the one named last changes fastest.
Arguments:
- hidden_in: bfloat16 [4096, 2304], P('dp'), may hold values from -6 to 6
- attn_gain: float32 [2304], replicated, may hold values from 0.25 to 1.75
- w_query: bfloat16 [2304, 2048], P(None, 'mp'), may hold values from -0.25 to 0.25
- w_key: bfloat16 [2304, 2048], P(None, 'mp'), may hold values from -0.125 to 0.125
- w_value: bfloat16 [2304, 2048], P(None, 'mp'), may hold values from -0.125 to 0.125
- w_out: bfloat16 [2048, 2304], P('mp'), may hold values from -0.5 to 0.5
- root_cache: bfloat16 [2, 4096, 2048], P(None, 'dp', 'mp'), may hold values from -400 to 400
- mid_cache: bfloat16 [2, 16, 1024, 2048], P(None, 'dp', None, 'mp'), may hold values from -400 to 400
- leaf_cache: bfloat16 [2, 32, 1024, 2048], P(None, 'dp', None, 'mp'), may hold values from -400 to 400
- mid_len: int32 [16], P('dp'), may hold values from 1 to 1024, 8192 in all
- leaf_len: int32 [32], P('dp'), may hold values from 1 to 1024, 16384 in all
- leaf_of: int32 [128], P('dp'), may hold values from 0 to 31, as said below
- parents: int32 [32], replicated, may hold values from 0 to 15, as said below
- suffix_len: int32 [128], P('dp'), may hold values from 1 to 32, 3072 in all
- ffn_gain: float32 [2304], replicated, may hold values from 0.25 to 1.75
- w_router: float32 [2304, 8], replicated, may hold values from -0.5 to 0.5
- routes: int32 [4096, 2], P('dp'), may hold values from 0 to 7, all different within a row; in each aligned block of 256 rows (0 to 255, 256 to 511, ...) at most 96 rows name the same one
- w_gate: bfloat16 [8, 2304, 5760], P('mp', None, 'dp'), may hold values from -0.125 to 0.125
- w_up: bfloat16 [8, 2304, 5760], P('mp', None, 'dp'), may hold values from -0.125 to 0.125
- w_down: bfloat16 [8, 5760, 2304], P('mp', 'dp'), may hold values from -0.078125 to 0.078125
Outputs:
- layer_out: bfloat16 [4096, 2304], P(('dp', 'mp'))
Inputs may be any that keep to these rules, and one draw needn't show every extreme that they name: `leaf_of`: leaf n belongs to index n // 2 of dp, mid-level node n to index n. The 8 sequences of one index of dp have different mid-level nodes and leaves of one parity, so that no two of them share a mid-level node or a leaf's owner. `parents`: every mid-level node is the parent of exactly one even and one odd leaf. `routes`: in the rows of one index of dp no expert is named by more than 96 rows; some indices of dp reach 96.
All inputs are finite; a program needn't handle non-finite values. No bound on the sum of `mid_len` or of `leaf_len` or of `suffix_len` on one device may be relied on, other than what follows from the above.
Results may differ from a plain program's by a relative error of at most 0.015.
The roundings to bfloat16 on the way count: a program that leaves them out, or rounds other values in their place, can miss the bound.
Values may be sent and summed in bfloat16 or wider, within the bound.
A program may use at most 128 MiB of HBM per device.

v0:
```python
import math
import jax
import jax.numpy as jnp
from jax import lax
from jax.sharding import PartitionSpec as P

HD = 64
TOP = 2
EPS = 1e-05
NEGATIVE = -1e30


def rms_scale(rows, gain):
    rows_wide = rows.astype(jnp.float32)
    mean_square = jnp.mean(rows_wide * rows_wide, axis=-1, keepdims=True)
    return rows_wide * lax.rsqrt(mean_square + EPS) * gain


def level_partial(queries, node_keys, node_values, limits, heads_here, batched):
    senders, row_count, width = queries.shape
    head_dim = width // heads_here
    scale = 1.0 / math.sqrt(head_dim)
    query_heads = queries.reshape(senders, row_count, heads_here, head_dim)
    if batched:
        key_heads = node_keys.reshape(senders, -1, heads_here, head_dim)
        value_heads = node_values.reshape(senders, -1, heads_here, head_dim)
        scores = jnp.einsum(
            "sqhd,skhd->sqhk", query_heads, key_heads, preferred_element_type=jnp.float32
        )
    else:
        key_heads = node_keys.reshape(-1, heads_here, head_dim)
        value_heads = node_values.reshape(-1, heads_here, head_dim)
        scores = jnp.einsum(
            "sqhd,khd->sqhk", query_heads, key_heads, preferred_element_type=jnp.float32
        )
    scores = scores * scale
    slots = jnp.arange(scores.shape[-1], dtype=jnp.int32)
    allowed = slots[None, :] < limits[:, None]
    scores = jnp.where(allowed[:, None, None, :], scores, NEGATIVE)
    peak = jnp.max(scores, axis=-1)
    weights = jnp.exp(scores - peak[..., None])
    total = jnp.sum(weights, axis=-1)
    probs = weights.astype(jnp.bfloat16)
    if batched:
        summed = jnp.einsum(
            "sqhk,skhd->sqhd", probs, value_heads, preferred_element_type=jnp.float32
        )
    else:
        summed = jnp.einsum(
            "sqhk,khd->sqhd", probs, value_heads, preferred_element_type=jnp.float32
        )
    result = (summed / total[..., None]).reshape(senders, row_count, width)
    return (result, peak + jnp.log(total))


def on_device(
    hidden_in,
    attn_gain,
    w_query,
    w_key,
    w_value,
    w_out,
    root_cache,
    mid_cache,
    leaf_cache,
    mid_len,
    leaf_len,
    leaf_of,
    parents,
    suffix_len,
    ffn_gain,
    w_router,
    routes,
    w_gate,
    w_up,
    w_down,
):
    tok_rows, width = hidden_in.shape
    seq_rows = suffix_len.shape[0]
    suffix = tok_rows // seq_rows
    head_dim = HD
    local_width = w_query.shape[1]
    heads_here = local_width // head_dim
    scale = 1.0 / math.sqrt(head_dim)
    owners = lax.axis_size("dp")
    normed = rms_scale(hidden_in, attn_gain).astype(jnp.bfloat16)
    query = jnp.dot(normed, w_query, preferred_element_type=jnp.float32).astype(jnp.bfloat16)
    key = jnp.dot(normed, w_key, preferred_element_type=jnp.float32).astype(jnp.bfloat16)
    value = jnp.dot(normed, w_value, preferred_element_type=jnp.float32).astype(jnp.bfloat16)
    query_heads = query.reshape(tok_rows, heads_here, head_dim)
    piece = lax.all_gather(root_cache, "dp", axis=1, tiled=True)
    running_peak = jnp.full((tok_rows, heads_here), NEGATIVE, jnp.float32)
    piece_keys = piece[0].reshape(-1, heads_here, head_dim)
    piece_values = piece[1].reshape(-1, heads_here, head_dim)
    scores = (
        jnp.einsum("qhd,khd->qhk", query_heads, piece_keys, preferred_element_type=jnp.float32)
        * scale
    )
    new_peak = jnp.maximum(running_peak, jnp.max(scores, axis=-1))
    weights = jnp.exp(scores - new_peak[..., None])
    new_total = jnp.sum(weights, axis=-1)
    added = jnp.einsum(
        "qhk,khd->qhd",
        weights.astype(jnp.bfloat16),
        piece_values,
        preferred_element_type=jnp.float32,
    )
    root_out = added / new_total[..., None]
    root_lse = new_peak + jnp.log(new_total)
    query_seq = query.reshape(seq_rows, suffix, heads_here, head_dim)
    key_seq = key.reshape(seq_rows, suffix, heads_here, head_dim)
    value_seq = value.reshape(seq_rows, suffix, heads_here, head_dim)
    slots = jnp.arange(suffix, dtype=jnp.int32)
    self_ok = (slots[None, None, :] <= slots[None, :, None]) & (
        slots[None, None, :] < suffix_len[:, None, None]
    )
    self_scores = (
        jnp.einsum("sqhd,skhd->sqhk", query_seq, key_seq, preferred_element_type=jnp.float32)
        * scale
    )
    self_scores = jnp.where(self_ok[:, :, None, :], self_scores, NEGATIVE)
    self_peak = jnp.max(self_scores, axis=-1)
    self_weights = jnp.exp(self_scores - self_peak[..., None])
    self_total = jnp.sum(self_weights, axis=-1)
    self_sum = jnp.einsum(
        "sqhk,skhd->sqhd",
        self_weights.astype(jnp.bfloat16),
        value_seq,
        preferred_element_type=jnp.float32,
    )
    self_out = (self_sum / self_total[..., None]).reshape(tok_rows, heads_here, head_dim)
    self_lse = (self_peak + jnp.log(self_total)).reshape(tok_rows, heads_here)
    mid_of = parents[leaf_of]
    leaf_owner = leaf_of // 2
    leaf_side = (leaf_of % 2).astype(jnp.float32)
    targets = jnp.arange(owners, dtype=jnp.int32)
    pick_mid = (mid_of[None, :] == targets[:, None]).astype(jnp.bfloat16)
    pick_leaf = (leaf_owner[None, :] == targets[:, None]).astype(jnp.bfloat16)
    flat_query = query.reshape(seq_rows, suffix * local_width)
    sent_mid = jnp.dot(pick_mid, flat_query, preferred_element_type=jnp.float32).astype(
        jnp.bfloat16
    )
    sent_leaf = jnp.dot(pick_leaf, flat_query, preferred_element_type=jnp.float32).astype(
        jnp.bfloat16
    )
    sent = jnp.stack([sent_mid, sent_leaf], axis=1).reshape(owners, 2, suffix, local_width)
    side_of_target = jnp.dot(
        pick_leaf.astype(jnp.float32), leaf_side, precision=lax.Precision.HIGHEST
    )
    sides = jnp.stack([jnp.zeros_like(side_of_target), side_of_target], axis=1)
    sides = jnp.broadcast_to(sides[:, :, None], (owners, 2, suffix)).astype(jnp.bfloat16)
    sent_queries = lax.all_to_all(sent, "dp", split_axis=0, concat_axis=0, tiled=True)
    sent_sides = lax.all_to_all(sides, "dp", split_axis=0, concat_axis=0, tiled=True)
    senders = sent_queries.shape[0]
    second = sent_sides[:, 1, 0] > 0.5
    mid_limit = jnp.broadcast_to(mid_len[0], (senders,))
    mid_result, mid_logsum = level_partial(
        sent_queries[:, 0], mid_cache[0, 0], mid_cache[1, 0], mid_limit, heads_here, False
    )
    leaf_keys = jnp.where(second[:, None, None], leaf_cache[0, 1][None], leaf_cache[0, 0][None])
    leaf_values = jnp.where(second[:, None, None], leaf_cache[1, 1][None], leaf_cache[1, 0][None])
    leaf_limit = jnp.where(second, leaf_len[1], leaf_len[0])
    leaf_result, leaf_logsum = level_partial(
        sent_queries[:, 1], leaf_keys, leaf_values, leaf_limit, heads_here, True
    )
    owner_out = jnp.stack([mid_result, leaf_result], axis=1)
    owner_lse = jnp.stack([mid_logsum, leaf_logsum], axis=1)
    back_out, back_lse = (
        lax.all_to_all(owner_out, "dp", split_axis=0, concat_axis=0, tiled=True),
        lax.all_to_all(owner_lse, "dp", split_axis=0, concat_axis=0, tiled=True),
    )
    mid_out = back_out[mid_of, 0].reshape(tok_rows, heads_here, head_dim)
    mid_lse = back_lse[mid_of, 0].reshape(tok_rows, heads_here)
    leaf_out = back_out[leaf_owner, 1].reshape(tok_rows, heads_here, head_dim)
    leaf_lse = back_lse[leaf_owner, 1].reshape(tok_rows, heads_here)
    stacked_lse = jnp.stack([root_lse, mid_lse, leaf_lse, self_lse])
    stacked_out = jnp.stack([root_out, mid_out, leaf_out, self_out])
    overall = jnp.max(stacked_lse, axis=0)
    shares = jnp.exp(stacked_lse - overall)
    combined = jnp.sum(shares[..., None] * stacked_out, axis=0) / jnp.sum(shares, axis=0)[..., None]
    attended = combined.reshape(tok_rows, local_width).astype(jnp.bfloat16)
    projected = jnp.dot(attended, w_out, preferred_element_type=jnp.float32)
    rows_here = tok_rows // lax.axis_size("mp")
    first = lax.axis_index("mp") * rows_here
    attn_all = lax.psum(projected, "mp")
    resid_all = hidden_in.astype(jnp.float32) + attn_all
    ffn_in = rms_scale(resid_all, ffn_gain).astype(jnp.bfloat16)
    resid = lax.dynamic_slice_in_dim(resid_all, first, rows_here, 0)
    logits = jnp.dot(ffn_in.astype(jnp.float32), w_router, precision=lax.Precision.HIGHEST)
    chosen = jnp.take_along_axis(logits, routes, axis=1)
    squashed = jax.nn.sigmoid(chosen)
    gates = squashed / jnp.sum(squashed, axis=1, keepdims=True)
    expert = lax.axis_index("mp")
    hit_each = routes == expert
    hit = jnp.any(hit_each, axis=1)
    gate_here = jnp.sum(jnp.where(hit_each, gates, 0.0), axis=1)
    order = jnp.cumsum(hit.astype(jnp.int32)) - 1
    capacity = 3 * TOP * tok_rows // (2 * lax.axis_size("mp"))
    slot_ids = jnp.arange(capacity, dtype=jnp.int32)
    pick_slot = (order[None, :] == slot_ids[:, None]) & hit[None, :]
    dispatch = jnp.dot(
        pick_slot.astype(jnp.bfloat16), ffn_in, preferred_element_type=jnp.float32
    ).astype(jnp.bfloat16)
    slot_gate = jnp.dot(pick_slot.astype(jnp.float32), gate_here, precision=lax.Precision.HIGHEST)
    gate_weight = w_gate[0]
    up_weight = w_up[0]
    down_weight = w_down[0]
    piece = lax.all_gather(dispatch, "dp", axis=0, tiled=True)
    gate_part = jnp.dot(piece, gate_weight, preferred_element_type=jnp.float32)
    up_part = jnp.dot(piece, up_weight, preferred_element_type=jnp.float32)
    partial_out = jnp.dot(
        (jax.nn.silu(gate_part) * up_part).astype(jnp.bfloat16),
        down_weight,
        preferred_element_type=jnp.float32,
    )
    expert_out = lax.psum_scatter(partial_out, "dp", scatter_dimension=0, tiled=True)
    weighted = expert_out * slot_gate[:, None]
    spread = jnp.dot(pick_slot.astype(jnp.float32).T, weighted, precision=lax.Precision.HIGHEST)
    mixed = lax.psum_scatter(spread, "mp", scatter_dimension=0, tiled=True)
    row_ids = first + jnp.arange(rows_here, dtype=jnp.int32)
    valid = row_ids % suffix < suffix_len[row_ids // suffix]
    return jnp.where(valid[:, None], resid + mixed, 0.0).astype(jnp.bfloat16)


def solution(mesh):
    return jax.shard_map(
        on_device,
        mesh=mesh,
        in_specs=(
            P("dp", None),
            P(),
            P(None, "mp"),
            P(None, "mp"),
            P(None, "mp"),
            P("mp", None),
            P(None, "dp", "mp"),
            P(None, "dp", None, "mp"),
            P(None, "dp", None, "mp"),
            P("dp"),
            P("dp"),
            P("dp"),
            P(),
            P("dp"),
            P(),
            P(),
            P("dp", None),
            P("mp", None, "dp"),
            P("mp", None, "dp"),
            P("mp", "dp", None),
        ),
        out_specs=P(("dp", "mp"), None),
        check_vma=False,
    )
```

profile of v0, /device:TPU:0, one launch (start us, length us, event | category | flops | bytes accessed | tf_op | source)
XLA Modules:
  0.0 482.1 jit_solution(8950069300431746591)
XLA Ops:
  9.6 8.1 %all-to-all-start.1 = ((bf16[16,2,32]{2,1,0:T(2,128)(2,1)}), bf16[16,2,32]{2,1,0:T(2,128)(2,1)S(1)}, u32[]{:S(2)}, u32[]{:S(2)}) async-start(bf16[16,2,32]{2,1,0:T(2,128)(2,1)} %broadcast_in_dim.168), calls=%async_computation.1 | async-start | bytes 16384 | tf_op jit(solution)/shard_map/all_to_all | solution.py:153
  34.5 7.6 %all-to-all-start = ((bf16[16,2,32,256]{3,2,1,0:T(8,128)(2,1)}), bf16[16,2,32,256]{3,2,1,0:T(8,128)(2,1)}, u32[]{:S(2)}, u32[]{:S(2)}) async-start(bf16[16,2,32,256]{3,2,1,0:T(8,128)(2,1)} %pad_maximum_fusion.1), calls=%async_computation | async-start | bytes 1048576 | tf_op jit(solution)/shard_map/all_to_all | solution.py:152
  62.5 4.5 bitcast_reduce_fusion.1
  69.3 2.7 fusion.64
  84.2 4.5 fusion.69
  93.0 7.1 %all-to-all-start.2 = ((f32[16,1,256]{2,1,0:T(1,128)}), f32[16,1,256]{2,1,0:T(1,128)S(1)}, u32[]{:S(2)}, u32[]{:S(2)}) async-start(f32[16,1,256]{2,1,0:T(1,128)} %reshape.482), calls=%async_computation.2 | async-start | bytes 32768 | tf_op jit(solution)/shard_map/all_to_all | solution.py:170
  102.3 5.3 %all-to-all-done.2 = f32[16,1,256]{2,1,0:T(1,128)S(1)} async-done(((f32[16,1,256]{2,1,0:T(1,128)}), f32[16,1,256]{2,1,0:T(1,128)S(1)}, u32[]{:S(2)}, u32[]{:S(2)}) %all-to-all-start.2) | async-done | bytes 16416 | tf_op jit(solution)/shard_map/all_to_all | solution.py:170
  107.7 4.3 all-to-all-start.3
  123.5 3.6 all-to-all-done.3
  136.3 4.5 fusion.133
  140.7 4.3 copy.247
  145.0 4.1 copy.269
  149.1 9.7 %bitcast_reduce_fusion = (f32[256,4]{0,1:T(4,128)S(1)}, f32[4,256,4096]{2,1,0:T(8,128)}) fusion(bf16[256,4,64]{0,2,1:T(8,128)(2,1)S(1)} %bitcast.204, bf16[4096,4,64]{0,2,1:T(8,128)(2,1)} %bitcast.186), kind=kOutput, calls=%fused_computation.8 | convolution fusion | flops 545258496 | bytes 19009536 | tf_op jit(solution)/shard_map/qhd,khd->qhk/dot_general | solution.py:96
  158.8 8.6 %fusion.2 = f32[256,4]{0,1:T(4,128)S(1)} fusion(f32[4,256,4096]{2,1,0:T(8,128)} %get-tuple-element.35, f32[256,4]{0,1:T(4,128)S(1)} %broadcast_maximum_fusion), kind=kLoop, calls=%fused_computation.11 | loop fusion | flops 12581888 | bytes 16785408 | tf_op jit(solution)/shard_map/reduce_sum | solution.py:101
  167.5 10.2 %fusion.60 = f32[1,256,4,64]{1,3,2,0:T(8,128)} fusion(bf16[4096,4,64]{0,2,1:T(8,128)(2,1)} %bitcast.188, f32[4,256,4096]{2,1,0:T(8,128)} %get-tuple-element.35, f32[256,4]{0,1:T(4,128)S(1)} %broadcast_maximum_fusion, f32[256,4]{0,1:T(4,128)S(1)} %fusion.2), kind=kOutput, calls=%fused_computation.76 | convolution fusion | flops 549519360 | bytes 19144704 | tf_op jit(solution)/shard_map/qhk,khd->qhd/dot_general | solution.py:102
  181.7 63.8 %all-reduce.5.cloned.1.call-done = f32[256,2304]{1,0:T(8,128)} async-done(((f32[256,2304]{1,0:T(8,128)}), f32[256,2304]{1,0:T(8,128)}) %all-reduce.5.cloned.1.call-update) | async-done | bytes 2359312 | tf_op jit(solution)/shard_map/psum | solution.py:185
  250.6 64.6 %all-gather.5.cloned.1.call-done = bf16[1536,2304]{1,0:T(8,128)(2,1)} async-done(((bf16[96,2304]{1,0:T(8,128)(2,1)}), bf16[1536,2304]{1,0:T(8,128)(2,1)}) %all-gather.5.cloned.1.call-update) | async-done | bytes 7077904 | tf_op jit(solution)/shard_map/all_gather | solution.py:208
  315.2 7.7 %fusion.36 = f32[1536,360]{0,1:T(8,128)} fusion(bf16[1536,2304]{1,0:T(8,128)(2,1)} %all-gather.5.cloned.1.call-done, bf16[1,2304,360]{1,2,0:T(8,128)(2,1)} %param.37), kind=kOutput, calls=%fused_computation.57 | convolution fusion | flops 2548039680 | bytes 10948608 | tf_op jit(solution)/shard_map/dot_general | solution.py:209
  322.8 14.3 %fusion.33 = f32[1536,2304]{1,0:T(8,128)} fusion(bf16[1,360,2304]{2,1,0:T(8,128)(2,1)S(1)} %copy-done, bf16[1536,2304]{1,0:T(8,128)(2,1)} %all-gather.5.cloned.1.call-done, f32[1536,360]{0,1:T(8,128)} %fusion.36, bf16[1,2304,360]{1,2,0:T(8,128)(2,1)} %param.38), kind=kOutput, calls=%fused_computation.54 | convolution fusion | flops 5099397120 | bytes 26763264 | tf_op jit(solution)/shard_map/dot_general | solution.py:211
  338.0 2.7 fusion.127
  340.7 3.6 gather_fusion.6
  344.7 92.1 %reduce-scatter.3.cloned.1.call-done = f32[96,2304]{1,0:T(8,128)} async-done(((f32[1536,2304]{1,0:T(8,128)}), f32[96,2304]{1,0:T(8,128)}) %reduce-scatter.3.cloned.1.call-update) | async-done | bytes 884752 | tf_op jit(solution)/shard_map/reduce_scatter | solution.py:216
  436.8 3.9 fusion.72
  441.4 32.1 %reduce-scatter.5.cloned.1.call-done = f32[32,2304]{1,0:T(8,128)} async-done(((f32[256,2304]{1,0:T(8,128)}), f32[32,2304]{1,0:T(8,128)}) %reduce-scatter.5.cloned.1.call-update) | async-done | bytes 294928 | tf_op jit(solution)/shard_map/reduce_scatter | solution.py:219
  (199 shorter events, 93.7 us)
Async XLA Ops:
  6.5 316.3 %copy-start = (bf16[1,360,2304]{2,1,0:T(8,128)(2,1)S(1)}, bf16[1,360,2304]{2,1,0:T(8,128)(2,1)}, u32[]{:S(2)}) copy-start(bf16[1,360,2304]{2,1,0:T(8,128)(2,1)} %param.39) | copy-start | bytes 4976644
  6.5 129.7 %all-gather.3.cloned.1.call-start = ((), (), s32[]{:S(2)}) async-start(), calls=%async_computation.6 | async-start | bytes 4456448 | tf_op jit(solution)/shard_map/all_gather | solution.py:91
  9.6 24.9 %all-to-all-start.1 = ((bf16[16,2,32]{2,1,0:T(2,128)(2,1)}), bf16[16,2,32]{2,1,0:T(2,128)(2,1)S(1)}, u32[]{:S(2)}, u32[]{:S(2)}) async-start(bf16[16,2,32]{2,1,0:T(2,128)(2,1)} %broadcast_in_dim.168), calls=%async_computation.1 | async-start | bytes 16384 | tf_op jit(solution)/shard_map/all_to_all | solution.py:153
  19.4 5.5 %copy-start.35 = (f32[256]{0:T(256)}, f32[256]{0:T(256)S(1)}, u32[]{:S(2)}) copy-start(f32[256]{0:T(256)S(1)} %add_rsqrt_fusion.1) | copy-start | bytes 3076
  26.9 4.9 %copy-start.7 = (bf16[2,2,1024,256]{3,2,1,0:T(8,128)(2,1)S(1)}, bf16[2,2,1024,256]{3,2,1,0:T(8,128)(2,1)}, u32[]{:S(2)}) copy-start(bf16[2,2,1024,256]{3,2,1,0:T(8,128)(2,1)} %param.28) | copy-start | bytes 6291460
  34.5 22.1 %all-to-all-start = ((bf16[16,2,32,256]{3,2,1,0:T(8,128)(2,1)}), bf16[16,2,32,256]{3,2,1,0:T(8,128)(2,1)}, u32[]{:S(2)}, u32[]{:S(2)}) async-start(bf16[16,2,32,256]{3,2,1,0:T(8,128)(2,1)} %pad_maximum_fusion.1), calls=%async_computation | async-start | bytes 1048576 | tf_op jit(solution)/shard_map/all_to_all | solution.py:152
  78.7 5.5 %copy-start.15 = (bf16[1,1,1024,256]{2,3,1,0:T(8,128)(2,1)S(1)}, bf16[1,1,1024,256]{2,3,1,0:T(8,128)(2,1)}, u32[]{:S(2)}) copy-start(bf16[1,1,1024,256]{2,3,1,0:T(8,128)(2,1)} %copy.270) | copy-start | bytes 1572868
  88.7 11.4 %copy-start.8 = (f32[16,1,32,256]{3,2,0,1:T(8,128)S(1)}, f32[16,1,32,256]{3,2,0,1:T(8,128)}, u32[]{:S(2)}) copy-start(f32[16,1,32,256]{3,2,0,1:T(8,128)} %stack_reshape.25) | copy-start | bytes 1572868
  93.0 19.1 %copy-start.25 = (f32[8,32,4]{1,2,0:T(4,128)S(1)}, f32[8,32,4]{1,2,0:T(4,128)}, u32[]{:S(2)}) copy-start(f32[8,32,4]{1,2,0:T(4,128)} %copy-done.24) | copy-start | bytes 12292
  93.0 19.1 %copy-start.26 = (f32[8,32,4]{1,2,0:T(4,128)S(1)}, f32[8,32,4]{1,2,0:T(4,128)}, u32[]{:S(2)}) copy-start(f32[8,32,4]{1,2,0:T(4,128)} %fusion.78) | copy-start | bytes 12292
  93.0 20.4 %copy-start.36 = (f32[256]{0:T(256)S(1)}, f32[256]{0:T(256)}, u32[]{:S(2)}) copy-start(f32[256]{0:T(256)} %copy-done.35) | copy-start | bytes 3076
  93.0 14.6 %all-to-all-start.2 = ((f32[16,1,256]{2,1,0:T(1,128)}), f32[16,1,256]{2,1,0:T(1,128)S(1)}, u32[]{:S(2)}, u32[]{:S(2)}) async-start(f32[16,1,256]{2,1,0:T(1,128)} %reshape.482), calls=%async_computation.2 | async-start | bytes 32768 | tf_op jit(solution)/shard_map/all_to_all | solution.py:170
  107.7 19.4 %all-to-all-start.3 = ((f32[16,2,32,256]{3,2,1,0:T(8,128)}), f32[16,2,32,256]{3,2,1,0:T(8,128)}, u32[]{:S(2)}, u32[]{:S(2)}) async-start(f32[16,2,32,256]{3,2,1,0:T(8,128)} %pad_maximum_fusion), calls=%async_computation.3 | async-start | bytes 2097152 | tf_op jit(solution)/shard_map/all_to_all | solution.py:169
  112.0 5.7 %copy-start.14 = (f32[8,32,4,32]{1,3,2,0:T(8,128)S(1)}, f32[8,32,4,32]{1,3,2,0:T(8,128)}, u32[]{:S(2)}) copy-start(f32[8,32,4,32]{1,3,2,0:T(8,128)} %copy-done.13) | copy-start | bytes 393220
  112.1 133.5 %all-reduce.5.cloned.1.call-start = ((), (), s32[]{:S(2)}) async-start(), calls=%async_computation.7 | async-start | bytes 4718592 | tf_op jit(solution)/shard_map/psum | solution.py:185
  167.4 10.2 %copy-start.31 = (f32[256,4]{0,1:T(4,128)S(1)}, f32[256,4]{0,1:T(4,128)}, u32[]{:S(2)}) copy-start(f32[256,4]{0,1:T(4,128)} %add.217) | copy-start | bytes 12292
  167.4 10.2 %copy-start.30 = (f32[1,256,4]{1,2,0:T(4,128)S(1)}, f32[1,256,4]{1,2,0:T(4,128)}, u32[]{:S(2)}) copy-start(f32[1,256,4]{1,2,0:T(4,128)} %add.216) | copy-start | bytes 12292
  167.4 10.3 %copy-start.11 = (f32[1,256,4,64]{1,3,2,0:T(8,128)S(1)}, f32[1,256,4,64]{1,3,2,0:T(8,128)}, u32[]{:S(2)}) copy-start(f32[1,256,4,64]{1,3,2,0:T(8,128)} %copy.282) | copy-start | bytes 786436
  167.4 10.3 %copy-start.12 = (f32[1,256,4,64]{1,3,2,0:T(8,128)S(1)}, f32[1,256,4,64]{1,3,2,0:T(8,128)}, u32[]{:S(2)}) copy-start(f32[1,256,4,64]{1,3,2,0:T(8,128)} %copy.281) | copy-start | bytes 786436
  181.0 134.1 %all-gather.5.cloned.1.call-start = ((), (), s32[]{:S(2)}) async-start(), calls=%async_computation.8 | async-start | bytes 7520256 | tf_op jit(solution)/shard_map/all_gather | solution.py:208
  181.7 67.4 %copy-start.28 = (f32[2304]{0:T(1024)S(1)}, f32[2304]{0:T(1024)}, u32[]{:S(2)}) copy-start(f32[2304]{0:T(1024)} %param.34) | copy-start | bytes 27652
  250.3 186.5 %reduce-scatter.3.cloned.1.call-start = ((), (), s32[]{:S(2)}) async-start(), calls=%async_computation.9 | async-start | bytes 15040512 | tf_op jit(solution)/shard_map/reduce_scatter | solution.py:216
  337.1 136.4 %reduce-scatter.5.cloned.1.call-start = ((), (), s32[]{:S(2)}) async-start(), calls=%async_computation.10 | async-start | bytes 2654208 | tf_op jit(solution)/shard_map/reduce_scatter | solution.py:219
  436.8 38.6 %copy-start.1 = (bf16[1,360,2304]{2,1,0:T(8,128)(2,1)S(1)}, bf16[1,360,2304]{2,1,0:T(8,128)(2,1)}, u32[]{:S(2)}) copy-start(bf16[1,360,2304]{2,1,0:T(8,128)(2,1)} %param.39) | copy-start | bytes 4976644
  (24 other events, 61.4 us)
Sparse Core Ops, SparseCore 0:
  9.6 59.1 all-gather.2
  181.1 64.3 all-reduce.4
  250.4 64.6 all-gather.4
  337.3 99.4 reduce-scatter.2
  440.8 32.7 reduce-scatter.4
where the time goes:
time: 487 us; the launch traced here: 482 us
  waiting for transfers between devices  263 us (54%)
  matrix products  76.3 us (16%)
  local copies, waits for them, and re-layouts  71.5 us (15%)
  other arithmetic  29.4 us (6%)
  starting transfers between devices  27.5 us (6%)
  between operations  14.7 us (3%)
    reduce_scatter x1, waiting for transfers between devices, on_device(): lax.psum_scatter(partial_out, 'dp', scatter_dimension=0, tiled=True)  92.1 us
    all_gather x1, waiting for transfers between devices, on_device(): piece = lax.all_gather(dispatch, 'dp', axis=0, tiled=True)  64.6 us
    psum x1, waiting for transfers between devices, on_device(): attn_all = lax.psum(projected, 'mp')  63.8 us
    reduce_scatter x1, waiting for transfers between devices, on_device(): mixed = lax.psum_scatter(spread, 'mp', scatter_dimension=0, tiled=True)  32.1 us
    dot_general x1, matrix products, on_device(): jnp.dot((jax.nn.silu(gate_part) * up_part).astype(jnp.bfloat16), down_wei...  14.3 us
    unnamed x87, local copies, waits for them, and re-layouts  13.6 us
    dot_general x1, matrix products, on_device(): jnp.einsum('qhk,khd->qhd', weights.astype(jnp.bfloat16), piece_values, pr...  10.2 us
  transfers between devices with their start and end apart: 9, of which 7 were waited for; matrix products, arithmetic and copies ran while one was open for 20% of the time, Pallas kernels for 0%

commit v1 on v0

--- a/solution.py
+++ b/solution.py
@@ -205,7 +205,8 @@
     gate_weight = w_gate[0]
     up_weight = w_up[0]
     down_weight = w_down[0]
-    piece = lax.all_gather(dispatch, "dp", axis=0, tiled=True)
+    outgoing = jnp.stack([dispatch] * lax.axis_size("dp"))
+    piece = jnp.concatenate(lax.all_to_all(outgoing, "dp", 0, 0), axis=0)
     gate_part = jnp.dot(piece, gate_weight, preferred_element_type=jnp.float32)
     up_part = jnp.dot(piece, up_weight, preferred_element_type=jnp.float32)
     partial_out = jnp.dot(

time: 487 us -> 508 us (1.043)
  blocking collectives: 0 us -> 86.7 us
  waiting for transfers between devices: 263 us -> 197 us
    all_to_all x0 -> x1, blocking collectives: none -> 86.7 us  [on_device(): piece = jnp.concatenate(lax.all_to_all(outgoing, 'dp', 0, 0), axis=0)]
    all_gather x1 -> x0, waiting for transfers between devices: 64.6 us -> none  [on_device(): piece = lax.all_gather(dispatch, 'dp', axis=0, tiled=True)]
    unnamed x87 -> x91, local copies, waits for them, and re-layouts: 13.6 us -> 16.4 us
  transfers between devices with their start and end apart: 9 -> 8, of which waited for: 7 -> 6; matrix products, arithmetic and copies ran while one was open for 20% -> 20% of each run, Pallas kernels for 0% -> 0%
where the time goes in v1:
time: 508 us; the launch traced here: 503 us
  waiting for transfers between devices  197 us (39%)
  blocking collectives  86.7 us (17%)
  local copies, waits for them, and re-layouts  75 us (15%)
  matrix products  72.1 us (14%)
  other arithmetic  29.5 us (6%)
  starting transfers between devices  27.5 us (5%)
  between operations  14.7 us (3%)
    reduce_scatter x1, waiting for transfers between devices, on_device(): lax.psum_scatter(partial_out, 'dp', scatter_dimension=0, tiled=True)  91.2 us
    all_to_all x1, blocking collectives, on_device(): piece = jnp.concatenate(lax.all_to_all(outgoing, 'dp', 0, 0), axis=0)  86.7 us
    psum x1, waiting for transfers between devices, on_device(): attn_all = lax.psum(projected, 'mp')  63.9 us
    reduce_scatter x1, waiting for transfers between devices, on_device(): mixed = lax.psum_scatter(spread, 'mp', scatter_dimension=0, tiled=True)  32.1 us
    unnamed x91, local copies, waits for them, and re-layouts  16.4 us
    dot_general x1, matrix products, on_device(): jnp.dot((jax.nn.silu(gate_part) * up_part).astype(jnp.bfloat16), down_wei...  14.3 us
    dot_general x1, matrix products, on_device(): jnp.einsum('qhk,khd->qhd', weights.astype(jnp.bfloat16), piece_values, pr...  10.2 us
  transfers between devices with their start and end apart: 8, of which 6 were waited for; matrix products, arithmetic and copies ran while one was open for 20% of the time, Pallas kernels for 0%

profile of v1, /device:TPU:0, one launch (start us, length us, event | category | flops | bytes accessed | tf_op | source)
XLA Modules:
  0.0 502.7 jit_solution(16222645508036659001)
XLA Ops:
  9.6 8.1 %all-to-all-start.1 = ((bf16[16,2,32]{2,1,0:T(2,128)(2,1)}), bf16[16,2,32]{2,1,0:T(2,128)(2,1)S(1)}, u32[]{:S(2)}, u32[]{:S(2)}) async-start(bf16[16,2,32]{2,1,0:T(2,128)(2,1)} %broadcast_in_dim.168), calls=%async_computation.1 | async-start | bytes 16384 | tf_op jit(solution)/shard_map/all_to_all | solution.py:153
  34.5 7.6 %all-to-all-start = ((bf16[16,2,32,256]{3,2,1,0:T(8,128)(2,1)}), bf16[16,2,32,256]{3,2,1,0:T(8,128)(2,1)}, u32[]{:S(2)}, u32[]{:S(2)}) async-start(bf16[16,2,32,256]{3,2,1,0:T(8,128)(2,1)} %pad_maximum_fusion.1), calls=%async_computation | async-start | bytes 1048576 | tf_op jit(solution)/shard_map/all_to_all | solution.py:152
  62.6 4.5 bitcast_reduce_fusion.1
  69.3 2.7 fusion.64
  84.2 4.5 fusion.69
  93.0 7.3 %all-to-all-start.2 = ((f32[16,1,256]{2,1,0:T(1,128)}), f32[16,1,256]{2,1,0:T(1,128)S(1)}, u32[]{:S(2)}, u32[]{:S(2)}) async-start(f32[16,1,256]{2,1,0:T(1,128)} %reshape.488), calls=%async_computation.2 | async-start | bytes 32768 | tf_op jit(solution)/shard_map/all_to_all | solution.py:170
  102.6 5.4 %all-to-all-done.2 = f32[16,1,256]{2,1,0:T(1,128)S(1)} async-done(((f32[16,1,256]{2,1,0:T(1,128)}), f32[16,1,256]{2,1,0:T(1,128)S(1)}, u32[]{:S(2)}, u32[]{:S(2)}) %all-to-all-start.2) | async-done | bytes 16416 | tf_op jit(solution)/shard_map/all_to_all | solution.py:170
  107.9 4.3 all-to-all-start.3
  123.8 3.5 all-to-all-done.3
  136.4 4.4 fusion.133
  140.8 4.3 copy.247
  145.1 4.1 copy.269
  149.2 9.7 %bitcast_reduce_fusion = (f32[256,4]{0,1:T(4,128)S(1)}, f32[4,256,4096]{2,1,0:T(8,128)}) fusion(bf16[256,4,64]{0,2,1:T(8,128)(2,1)S(1)} %bitcast.207, bf16[4096,4,64]{0,2,1:T(8,128)(2,1)} %bitcast.187), kind=kOutput, calls=%fused_computation.8 | convolution fusion | flops 545258496 | bytes 19009536 | tf_op jit(solution)/shard_map/qhd,khd->qhk/dot_general | solution.py:96
  158.9 8.6 %fusion.2 = f32[256,4]{0,1:T(4,128)S(1)} fusion(f32[4,256,4096]{2,1,0:T(8,128)} %get-tuple-element.35, f32[256,4]{0,1:T(4,128)S(1)} %broadcast_maximum_fusion), kind=kLoop, calls=%fused_computation.11 | loop fusion | flops 12581888 | bytes 16785408 | tf_op jit(solution)/shard_map/reduce_sum | solution.py:101
  167.6 10.2 %fusion.60 = f32[1,256,4,64]{1,3,2,0:T(8,128)} fusion(bf16[4096,4,64]{0,2,1:T(8,128)(2,1)} %bitcast.191, f32[4,256,4096]{2,1,0:T(8,128)} %get-tuple-element.35, f32[256,4]{0,1:T(4,128)S(1)} %broadcast_maximum_fusion, f32[256,4]{0,1:T(4,128)S(1)} %fusion.2), kind=kOutput, calls=%fused_computation.76 | convolution fusion | flops 549519360 | bytes 19144704 | tf_op jit(solution)/shard_map/qhk,khd->qhd/dot_general | solution.py:102
  181.8 63.9 %all-reduce.5.cloned.1.call-done = f32[256,2304]{1,0:T(8,128)} async-done(((f32[256,2304]{1,0:T(8,128)}), f32[256,2304]{1,0:T(8,128)}) %all-reduce.5.cloned.1.call-update) | async-done | bytes 2359312 | tf_op jit(solution)/shard_map/psum | solution.py:185
  250.5 86.7 %all_to_all.25 = bf16[16,96,2304]{2,1,0:T(8,128)(2,1)S(1)} all-to-all(bf16[16,96,2304]{2,1,0:T(8,128)(2,1)S(1)} %stack.69), channel_id=1, replica_groups=mesh['dp'=16,'mp'=8] {'dp'}, dimensions={0} | all-to-all | bytes 14155776 | tf_op jit(solution)/shard_map/all_to_all | solution.py:209
  337.2 2.8 copy-done.6
  340.0 4.2 fusion.36
  344.3 14.3 %fusion.33 = f32[1536,2304]{1,0:T(8,128)} fusion(bf16[1,360,2304]{2,1,0:T(8,128)(2,1)S(1)} %copy-done, bf16[1536,2304]{1,0:T(8,128)(2,1)} %bitcast.189, f32[1536,360]{0,1:T(8,128)} %fusion.36, bf16[1,2304,360]{1,2,0:T(8,128)(2,1)} %param.38), kind=kOutput, calls=%fused_computation.54 | convolution fusion | flops 5099397120 | bytes 26763264 | tf_op jit(solution)/shard_map/dot_general | solution.py:212
  362.2 3.6 gather_fusion.6
  366.1 91.2 %reduce-scatter.3.cloned.1.call-done = f32[96,2304]{1,0:T(8,128)} async-done(((f32[1536,2304]{1,0:T(8,128)}), f32[96,2304]{1,0:T(8,128)}) %reduce-scatter.3.cloned.1.call-update) | async-done | bytes 884752 | tf_op jit(solution)/shard_map/reduce_scatter | solution.py:217
  457.3 3.9 fusion.72
  462.0 32.1 %reduce-scatter.5.cloned.1.call-done = f32[32,2304]{1,0:T(8,128)} async-done(((f32[256,2304]{1,0:T(8,128)}), f32[32,2304]{1,0:T(8,128)}) %reduce-scatter.5.cloned.1.call-update) | async-done | bytes 294928 | tf_op jit(solution)/shard_map/reduce_scatter | solution.py:220
  (202 shorter events, 96.1 us)
Async XLA Ops:
  6.5 337.7 %copy-start = (bf16[1,360,2304]{2,1,0:T(8,128)(2,1)S(1)}, bf16[1,360,2304]{2,1,0:T(8,128)(2,1)}, u32[]{:S(2)}) copy-start(bf16[1,360,2304]{2,1,0:T(8,128)(2,1)} %param.39) | copy-start | bytes 4976644
  6.5 129.9 %all-gather.2.cloned.1.call-start = ((), (), s32[]{:S(2)}) async-start(), calls=%async_computation.7 | async-start | bytes 4456448 | tf_op jit(solution)/shard_map/all_gather | solution.py:91
  9.6 24.9 %all-to-all-start.1 = ((bf16[16,2,32]{2,1,0:T(2,128)(2,1)}), bf16[16,2,32]{2,1,0:T(2,128)(2,1)S(1)}, u32[]{:S(2)}, u32[]{:S(2)}) async-start(bf16[16,2,32]{2,1,0:T(2,128)(2,1)} %broadcast_in_dim.168), calls=%async_computation.1 | async-start | bytes 16384 | tf_op jit(solution)/shard_map/all_to_all | solution.py:153
  19.4 5.4 %copy-start.36 = (f32[256]{0:T(256)}, f32[256]{0:T(256)S(1)}, u32[]{:S(2)}) copy-start(f32[256]{0:T(256)S(1)} %add_rsqrt_fusion.1) | copy-start | bytes 3076
  26.9 4.9 copy-start.8
  34.5 22.1 %all-to-all-start = ((bf16[16,2,32,256]{3,2,1,0:T(8,128)(2,1)}), bf16[16,2,32,256]{3,2,1,0:T(8,128)(2,1)}, u32[]{:S(2)}, u32[]{:S(2)}) async-start(bf16[16,2,32,256]{3,2,1,0:T(8,128)(2,1)} %pad_maximum_fusion.1), calls=%async_computation | async-start | bytes 1048576 | tf_op jit(solution)/shard_map/all_to_all | solution.py:152
  78.7 5.4 %copy-start.16 = (bf16[1,1,1024,256]{2,3,1,0:T(8,128)(2,1)S(1)}, bf16[1,1,1024,256]{2,3,1,0:T(8,128)(2,1)}, u32[]{:S(2)}) copy-start(bf16[1,1,1024,256]{2,3,1,0:T(8,128)(2,1)} %copy.270) | copy-start | bytes 1572868
  88.7 11.7 %copy-start.9 = (f32[16,1,32,256]{3,2,0,1:T(8,128)S(1)}, f32[16,1,32,256]{3,2,0,1:T(8,128)}, u32[]{:S(2)}) copy-start(f32[16,1,32,256]{3,2,0,1:T(8,128)} %stack_reshape.25) | copy-start | bytes 1572868
  93.0 19.3 %copy-start.26 = (f32[8,32,4]{1,2,0:T(4,128)S(1)}, f32[8,32,4]{1,2,0:T(4,128)}, u32[]{:S(2)}) copy-start(f32[8,32,4]{1,2,0:T(4,128)} %copy-done.25) | copy-start | bytes 12292
  93.0 19.3 %copy-start.27 = (f32[8,32,4]{1,2,0:T(4,128)S(1)}, f32[8,32,4]{1,2,0:T(4,128)}, u32[]{:S(2)}) copy-start(f32[8,32,4]{1,2,0:T(4,128)} %fusion.78) | copy-start | bytes 12292
  93.0 20.7 %copy-start.37 = (f32[256]{0:T(256)S(1)}, f32[256]{0:T(256)}, u32[]{:S(2)}) copy-start(f32[256]{0:T(256)} %copy-done.36) | copy-start | bytes 3076
  93.0 14.9 %all-to-all-start.2 = ((f32[16,1,256]{2,1,0:T(1,128)}), f32[16,1,256]{2,1,0:T(1,128)S(1)}, u32[]{:S(2)}, u32[]{:S(2)}) async-start(f32[16,1,256]{2,1,0:T(1,128)} %reshape.488), calls=%async_computation.2 | async-start | bytes 32768 | tf_op jit(solution)/shard_map/all_to_all | solution.py:170
  107.9 19.3 %all-to-all-start.3 = ((f32[16,2,32,256]{3,2,1,0:T(8,128)}), f32[16,2,32,256]{3,2,1,0:T(8,128)}, u32[]{:S(2)}, u32[]{:S(2)}) async-start(f32[16,2,32,256]{3,2,1,0:T(8,128)} %pad_maximum_fusion), calls=%async_computation.3 | async-start | bytes 2097152 | tf_op jit(solution)/shard_map/all_to_all | solution.py:169
  112.3 5.7 %copy-start.15 = (f32[8,32,4,32]{1,3,2,0:T(8,128)S(1)}, f32[8,32,4,32]{1,3,2,0:T(8,128)}, u32[]{:S(2)}) copy-start(f32[8,32,4,32]{1,3,2,0:T(8,128)} %copy-done.14) | copy-start | bytes 393220
  112.3 133.5 %all-reduce.5.cloned.1.call-start = ((), (), s32[]{:S(2)}) async-start(), calls=%async_computation.8 | async-start | bytes 4718592 | tf_op jit(solution)/shard_map/psum | solution.py:185
  167.5 10.2 %copy-start.32 = (f32[256,4]{0,1:T(4,128)S(1)}, f32[256,4]{0,1:T(4,128)}, u32[]{:S(2)}) copy-start(f32[256,4]{0,1:T(4,128)} %add.217) | copy-start | bytes 12292
  167.5 10.2 %copy-start.31 = (f32[1,256,4]{1,2,0:T(4,128)S(1)}, f32[1,256,4]{1,2,0:T(4,128)}, u32[]{:S(2)}) copy-start(f32[1,256,4]{1,2,0:T(4,128)} %add.216) | copy-start | bytes 12292
  167.6 10.3 %copy-start.12 = (f32[1,256,4,64]{1,3,2,0:T(8,128)S(1)}, f32[1,256,4,64]{1,3,2,0:T(8,128)}, u32[]{:S(2)}) copy-start(f32[1,256,4,64]{1,3,2,0:T(8,128)} %copy.282) | copy-start | bytes 786436
  167.6 10.3 %copy-start.13 = (f32[1,256,4,64]{1,3,2,0:T(8,128)S(1)}, f32[1,256,4,64]{1,3,2,0:T(8,128)}, u32[]{:S(2)}) copy-start(f32[1,256,4,64]{1,3,2,0:T(8,128)} %copy.281) | copy-start | bytes 786436
  181.1 276.2 %reduce-scatter.3.cloned.1.call-start = ((), (), s32[]{:S(2)}) async-start(), calls=%async_computation.9 | async-start | bytes 15040512 | tf_op jit(solution)/shard_map/reduce_scatter | solution.py:217
  181.8 67.5 %copy-start.29 = (f32[2304]{0:T(1024)S(1)}, f32[2304]{0:T(1024)}, u32[]{:S(2)}) copy-start(f32[2304]{0:T(1024)} %param.34) | copy-start | bytes 27652
  250.5 89.6 %copy-start.39 = (bf16[1,2304,360]{1,2,0:T(8,128)(2,1)S(1)}, bf16[1,2304,360]{1,2,0:T(8,128)(2,1)}, u32[]{:S(2)}) copy-start(bf16[1,2304,360]{1,2,0:T(8,128)(2,1)} %param.37) | copy-start | bytes 4976644
  358.6 135.6 %reduce-scatter.5.cloned.1.call-start = ((), (), s32[]{:S(2)}) async-start(), calls=%async_computation.10 | async-start | bytes 2654208 | tf_op jit(solution)/shard_map/reduce_scatter | solution.py:220
  457.3 38.6 %copy-start.1 = (bf16[1,360,2304]{2,1,0:T(8,128)(2,1)S(1)}, bf16[1,360,2304]{2,1,0:T(8,128)(2,1)}, u32[]{:S(2)}) copy-start(bf16[1,360,2304]{2,1,0:T(8,128)(2,1)} %param.39) | copy-start | bytes 4976644
  (25 other events, 64.2 us)
Sparse Core Ops, SparseCore 0:
  9.6 59.0 all-gather.1
  181.2 64.4 all-reduce.4
  358.7 98.5 reduce-scatter.2
  461.3 32.7 reduce-scatter.4
